TPU v7x, 512 devices: a whole 4x8x8 slice. The times are simulated.
512 devices in a mesh: row: 32 (over x, y), col: 8 (over z_hi, core), vec: 2 (over z_lo).
Axes of the slice: x: 4, y: 8, z: 8 (z_hi: 4, z_lo: 2; z = z_hi * 2 + z_lo), core: 2. Of those that a mesh axis runs over, the one named last changes fastest.
Arguments:
- vectors: bfloat16 [131072, 256], P(('row', 'col'), 'vec'), parts along dimension 1, may hold values from -6 to 6
- tile_blocks: bfloat16 [32, 8, 32, 256, 256], P('row', 'col'), may hold values from -0.125 to 0.125
- block_rows: int32 [32, 8, 32], P('row', 'col'), may hold values from 0 to 15, as said below
- block_cols: int32 [32, 8, 32], P('row', 'col'), may hold values from 0 to 63, as said below
- counts: int32 [32, 8], P('row', 'col'), may hold values from 1 to 32, as said below
Outputs:
- filtered: bfloat16 [131072, 256], P(('row', 'col'), 'vec'), parts along dimension 1
There are 2 independent parts, one for each index of `vec`. A program takes and returns all parts, laid end to end along the dimension named above; an argument that names none is the same for every part. Nothing has to cross between parts.
Inputs may be any that keep to these rules, and one draw needn't show every extreme that they name: The pairs (block_rows, block_cols // 2) of the 32 slots of one tile are all distinct. Within one tile, all slots whose block columns lie in the same group of 2 (same block_cols // 2) name the same block column. `counts`: some tile uses all 32 slots.
All inputs are finite; a program needn't handle non-finite values.
Results may differ from a plain program's by a relative error of at most 0.015.
Values may be sent and summed in bfloat16 or wider, within the bound.
A program may use at most 64 MiB of HBM per device.

v0:
```python
import jax
import jax.numpy as jnp
from jax import lax
from jax.sharding import PartitionSpec as P

DEGREE = 3
center_value = 0.5
half_width = 2.0


def on_device(vectors, tile_blocks, block_rows, block_cols, counts):
    n_row = lax.axis_size("row")
    n_col = lax.axis_size("col")
    tile_data = tile_blocks[0, 0]
    slot_rows = block_rows[0, 0]
    slot_cols = block_cols[0, 0]
    used = counts[0, 0]
    block_size = tile_data.shape[-1]
    width = vectors.shape[1]
    piece_blocks = vectors.shape[0] // block_size
    row_blocks = piece_blocks * n_col
    slot_count = tile_data.shape[0]
    live = (jnp.arange(slot_count) < used).astype(jnp.float32)
    onehot = (slot_rows[None, :] == jnp.arange(row_blocks)[:, None]).astype(jnp.float32) * live[
        None, :
    ]

    def apply_tiles(current):
        gathered = lax.all_gather(current, "row", axis=0, tiled=True)
        vec_blocks = jnp.take(
            gathered.reshape(n_row * piece_blocks, block_size, width), slot_cols, axis=0
        )
        products = jnp.einsum(
            "sij,sjk->sik", tile_data, vec_blocks, preferred_element_type=jnp.float32
        )
        term = jnp.einsum("ls,sik->lik", onehot, products, precision=lax.Precision.HIGHEST)
        term = term.reshape(row_blocks * block_size, width)
        return lax.psum_scatter(
            term.astype(jnp.bfloat16), "col", scatter_dimension=0, tiled=True
        ).astype(jnp.float32)

    previous = vectors
    applied = apply_tiles(vectors)
    current = ((applied - center_value * previous.astype(jnp.float32)) / half_width).astype(
        jnp.bfloat16
    )
    for repeat in range(DEGREE - 1):
        applied = apply_tiles(current)
        following = (
            2.0 * (applied - center_value * current.astype(jnp.float32)) / half_width
            - previous.astype(jnp.float32)
        ).astype(jnp.bfloat16)
        previous, current = (current, following)
    return current


def solution(mesh):
    return jax.shard_map(
        on_device,
        mesh=mesh,
        in_specs=(
            P(("row", "col"), "vec"),
            P("row", "col", None, None, None),
            P("row", "col", None),
            P("row", "col", None),
            P("row", "col"),
        ),
        out_specs=P(("row", "col"), "vec"),
        check_vma=False,
    )
```

profile of v0, /device:TPU:2, one launch (start us, length us, event | category | flops | bytes accessed | tf_op | source)
XLA Modules:
  0.0 470.1 jit_solution(5632547068831693479)
XLA Ops:
  9.3 91.6 %all-gather.4.cloned.1.call-done = bf16[16384,128]{1,0:T(8,128)(2,1)} async-done(((bf16[512,128]{1,0:T(8,128)(2,1)}), bf16[16384,128]{1,0:T(8,128)(2,1)}) %all-gather.4.cloned.1.call-update) | async-done | bytes 4194320 | tf_op jit(solution)/shard_map/all_gather | solution.py:29
  100.9 3.1 gather_fusion
  104.1 6.6 %fusion.10 = f32[32,128,256]{2,1,0:T(8,128)} fusion(bf16[1,1,32,256,256]{4,3,2,1,0:T(8,128)(2,1)} %param.8, bf16[32,256,128]{2,1,0:T(8,128)(2,1)S(1)} %gather_fusion, pred[32]{0:T(512)(128)(4,1)S(1)} %compare_and_fusion), kind=kOutput, calls=%fused_computation.13 | convolution fusion | flops 537919488 | bytes 10485792 | tf_op jit(solution)/shard_map/sij,sjk->sik/dot_general | solution.py:33
  110.6 5.5 %copy.9 = f32[32,128,256]{1,0,2:T(8,128)} copy(f32[32,128,256]{2,1,0:T(8,128)} %fusion.10) | data formatting | bytes 8388608 | tf_op jit(solution)/shard_map/sij,sjk->sik/dot_general | solution.py:33
  116.2 4.3 fusion.18
  120.5 1.2 copy.6
  121.8 41.6 %reduce-scatter.4.cloned.1.call-done = bf16[512,128]{1,0:T(8,128)(2,1)} async-done(((bf16[4096,128]{1,0:T(8,128)(2,1)}), bf16[512,128]{1,0:T(8,128)(2,1)}) %reduce-scatter.4.cloned.1.call-update) | async-done | bytes 131088 | tf_op jit(solution)/shard_map/reduce_scatter | solution.py:38
  163.4 1.6 fusion.32
  165.1 84.9 %all-gather.6.cloned.1.call-done = bf16[16384,128]{1,0:T(8,128)(2,1)} async-done(((bf16[512,128]{1,0:T(8,128)(2,1)}), bf16[16384,128]{1,0:T(8,128)(2,1)}) %all-gather.6.cloned.1.call-update) | async-done | bytes 4194320 | tf_op jit(solution)/shard_map/all_gather | solution.py:29
  250.0 3.1 gather_fusion.1
  253.1 6.6 %fusion.8 = f32[32,128,256]{2,1,0:T(8,128)} fusion(bf16[1,1,32,256,256]{4,3,2,1,0:T(8,128)(2,1)} %param.8, bf16[32,256,128]{2,1,0:T(8,128)(2,1)S(1)} %gather_fusion.1, pred[32]{0:T(512)(128)(4,1)S(1)} %compare_and_fusion), kind=kOutput, calls=%fused_computation.11 | convolution fusion | flops 537919488 | bytes 10485792 | tf_op jit(solution)/shard_map/sij,sjk->sik/dot_general | solution.py:33
  259.7 5.5 %copy.10 = f32[32,128,256]{1,0,2:T(8,128)} copy(f32[32,128,256]{2,1,0:T(8,128)} %fusion.8) | data formatting | bytes 8388608 | tf_op jit(solution)/shard_map/sij,sjk->sik/dot_general | solution.py:33
  265.2 4.3 fusion.21
  269.5 1.2 copy.7
  270.9 41.7 %reduce-scatter.6.cloned.1.call-done = bf16[512,128]{1,0:T(8,128)(2,1)} async-done(((bf16[4096,128]{1,0:T(8,128)(2,1)}), bf16[512,128]{1,0:T(8,128)(2,1)}) %reduce-scatter.6.cloned.1.call-update) | async-done | bytes 131088 | tf_op jit(solution)/shard_map/reduce_scatter | solution.py:38
  312.6 1.6 fusion.33
  314.4 84.6 %all-gather.8.cloned.1.call-done = bf16[16384,128]{1,0:T(8,128)(2,1)} async-done(((bf16[512,128]{1,0:T(8,128)(2,1)}), bf16[16384,128]{1,0:T(8,128)(2,1)}) %all-gather.8.cloned.1.call-update) | async-done | bytes 4194320 | tf_op jit(solution)/shard_map/all_gather | solution.py:29
  399.0 3.1 gather_fusion.2
  402.2 6.6 %fusion.6 = f32[32,128,256]{2,1,0:T(8,128)} fusion(bf16[1,1,32,256,256]{4,3,2,1,0:T(8,128)(2,1)} %param.8, bf16[32,256,128]{2,1,0:T(8,128)(2,1)S(1)} %gather_fusion.2, pred[32]{0:T(512)(128)(4,1)S(1)} %compare_and_fusion), kind=kOutput, calls=%fused_computation.9 | convolution fusion | flops 537919488 | bytes 10485792 | tf_op jit(solution)/shard_map/sij,sjk->sik/dot_general | solution.py:33
  408.8 5.5 %copy.11 = f32[32,128,256]{1,0,2:T(8,128)} copy(f32[32,128,256]{2,1,0:T(8,128)} %fusion.6) | data formatting | bytes 8388608 | tf_op jit(solution)/shard_map/sij,sjk->sik/dot_general | solution.py:33
  414.3 4.3 fusion.24
  418.6 1.2 copy.8
  419.9 41.7 %reduce-scatter.8.cloned.1.call-done = bf16[512,128]{1,0:T(8,128)(2,1)} async-done(((bf16[4096,128]{1,0:T(8,128)(2,1)}), bf16[512,128]{1,0:T(8,128)(2,1)}) %reduce-scatter.8.cloned.1.call-update) | async-done | bytes 131088 | tf_op jit(solution)/shard_map/reduce_scatter | solution.py:38
  461.6 1.6 fusion.35
  (24 shorter events, 2.5 us)
Async XLA Ops:
  6.5 94.4 %all-gather.4.cloned.1.call-start = ((), (), s32[]{:S(2)}) async-start(), calls=%async_computation.3 | async-start | bytes 4325376 | tf_op jit(solution)/shard_map/all_gather | solution.py:29
  7.3 156.2 %reduce-scatter.4.cloned.1.call-start = ((), (), s32[]{:S(2)}) async-start(), calls=%async_computation.4 | async-start | bytes 1179648 | tf_op jit(solution)/shard_map/reduce_scatter | solution.py:38
  110.6 5.5 %copy-start.3 = (s32[1,1,32]{2,1,0:T(1,128)S(1)}, s32[1,1,32]{2,1,0:T(1,128)}, u32[]{:S(2)}) copy-start(s32[1,1,32]{2,1,0:T(1,128)} %param.9) | copy-start | bytes 388
  116.2 47.2 %copy-start.1 = (bf16[512,128]{1,0:T(8,128)(2,1)S(1)}, bf16[512,128]{1,0:T(8,128)(2,1)}, u32[]{:S(2)}) copy-start(bf16[512,128]{1,0:T(8,128)(2,1)} %param.7) | copy-start | bytes 393220
  121.8 128.2 %all-gather.6.cloned.1.call-start = ((), (), s32[]{:S(2)}) async-start(), calls=%async_computation.5 | async-start | bytes 4325376 | tf_op jit(solution)/shard_map/all_gather | solution.py:29
  165.1 147.5 %reduce-scatter.6.cloned.1.call-start = ((), (), s32[]{:S(2)}) async-start(), calls=%async_computation.6 | async-start | bytes 1179648 | tf_op jit(solution)/shard_map/reduce_scatter | solution.py:38
  265.2 47.3 %copy-start = (bf16[512,128]{1,0:T(8,128)(2,1)S(1)}, bf16[512,128]{1,0:T(8,128)(2,1)}, u32[]{:S(2)}) copy-start(bf16[512,128]{1,0:T(8,128)(2,1)} %fusion.32) | copy-start | bytes 393220
  270.8 128.2 %all-gather.8.cloned.1.call-start = ((), (), s32[]{:S(2)}) async-start(), calls=%async_computation.7 | async-start | bytes 4325376 | tf_op jit(solution)/shard_map/all_gather | solution.py:29
  314.2 147.4 %reduce-scatter.8.cloned.1.call-start = ((), (), s32[]{:S(2)}) async-start(), calls=%async_computation.8 | async-start | bytes 1179648 | tf_op jit(solution)/shard_map/reduce_scatter | solution.py:38
  414.3 47.3 %copy-start.2 = (bf16[512,128]{1,0:T(8,128)(2,1)S(1)}, bf16[512,128]{1,0:T(8,128)(2,1)}, u32[]{:S(2)}) copy-start(bf16[512,128]{1,0:T(8,128)(2,1)} %fusion.33) | copy-start | bytes 393220
Sparse Core Ops, SparseCore 0:
  10.5 90.3 all-gather.3
  121.9 41.4 reduce-scatter.3
  166.6 83.3 all-gather.5
  270.9 41.5 reduce-scatter.5
  315.6 83.4 all-gather.7
  420.0 41.5 reduce-scatter.7
where the time goes:
time: 471 us; the launch traced here: 470 us
  waiting for transfers between devices  387 us (82%)
  matrix products  32.6 us (7%)
  local copies, waits for them, and re-layouts  29.7 us (6%)
  between operations  14.2 us (3%)
  other arithmetic  6.19 us (1%)
    all_gather x3, waiting for transfers between devices, apply_tiles(): gathered = lax.all_gather(current, 'row', axis=0, tiled=True)  261 us
    reduce_scatter x3, waiting for transfers between devices, apply_tiles(): lax.psum_scatter(term.astype(jnp.bfloat16), 'col', scatter_dimension=0, t...  125 us
    dot_general x3, matrix products, apply_tiles(): jnp.einsum('sij,sjk->sik', tile_data, vec_blocks, preferred_element_type=...  19.7 us
    dot_general x3, local copies, waits for them, and re-layouts, apply_tiles(): jnp.einsum('sij,sjk->sik', tile_data, vec_blocks, preferred_element_type=...  16.5 us
    dot_general x3, matrix products, apply_tiles(): jnp.einsum('ls,sik->lik', onehot, products, precision=lax.Precision.HIGHEST)  12.9 us
  transfers between devices with their start and end apart: 6, of which 6 were waited for; matrix products, arithmetic and copies ran while one was open for 0% of the time, Pallas kernels for 0%

commit v1 on v0

--- a/solution.py
+++ b/solution.py
@@ -26,7 +26,9 @@
     ]
 
     def apply_tiles(current):
-        gathered = lax.all_gather(current, "row", axis=0, tiled=True)
+        gathered = jnp.concatenate(
+            lax.all_to_all(jnp.stack([current] * lax.axis_size("row")), "row", 0, 0), axis=0
+        )
         vec_blocks = jnp.take(
             gathered.reshape(n_row * piece_blocks, block_size, width), slot_cols, axis=0
         )

time: 471 us -> 518 us (1.100)
  the two profiles are of different devices: /device:TPU:2 before, /device:TPU:4 now
where the time goes in v1:
time: 518 us; the launch traced here: 517 us
  waiting for transfers between devices  218 us (42%)
  blocking collectives  203 us (39%)
  local copies, waits for them, and re-layouts  35.3 us (7%)
  matrix products  32.5 us (6%)
  between operations  13.9 us (3%)
  starting transfers between devices  10.8 us (2%)
    all_to_all x2, blocking collectives, apply_tiles(): lax.all_to_all(jnp.stack([current] * lax.axis_size('row')), 'row', 0, 0)  203 us
    reduce_scatter x3, waiting for transfers between devices, apply_tiles(): lax.psum_scatter(term.astype(jnp.bfloat16), 'col', scatter_dimension=0, t...  124 us
    all_to_all x1, waiting for transfers between devices, apply_tiles(): lax.all_to_all(jnp.stack([current] * lax.axis_size('row')), 'row', 0, 0)  93.8 us
    dot_general x3, matrix products, apply_tiles(): jnp.einsum('sij,sjk->sik', tile_data, vec_blocks, preferred_element_type=...  19.7 us
    dot_general x3, local copies, waits for them, and re-layouts, apply_tiles(): jnp.einsum('sij,sjk->sik', tile_data, vec_blocks, preferred_element_type=...  16.5 us
    dot_general x3, matrix products, apply_tiles(): jnp.einsum('ls,sik->lik', onehot, products, precision=lax.Precision.HIGHEST)  12.9 us
    all_to_all x1, starting transfers between devices, apply_tiles(): lax.all_to_all(jnp.stack([current] * lax.axis_size('row')), 'row', 0, 0)  10.5 us
  transfers between devices with their start and end apart: 4, of which 4 were waited for; matrix products, arithmetic and copies ran while one was open for 0% of the time, Pallas kernels for 0%

profile of v1, /device:TPU:4, one launch (start us, length us, event | category | flops | bytes accessed | tf_op | source)
XLA Modules:
  0.0 517.5 jit_solution(16131196851127831485)
XLA Ops:
  6.5 3.8 stack.6
  10.4 10.5 %all-to-all-start = ((bf16[32,512,128]{2,1,0:T(8,128)(2,1)}), bf16[32,512,128]{2,1,0:T(8,128)(2,1)}, u32[]{:S(2)}, u32[]{:S(2)}) async-start(bf16[32,512,128]{2,1,0:T(8,128)(2,1)} %stack.6), calls=%async_computation | async-start | bytes 8388608 | tf_op jit(solution)/shard_map/all_to_all | solution.py:30
  21.6 93.8 %all-to-all-done = bf16[32,512,128]{2,1,0:T(8,128)(2,1)} async-done(((bf16[32,512,128]{2,1,0:T(8,128)(2,1)}), bf16[32,512,128]{2,1,0:T(8,128)(2,1)}, u32[]{:S(2)}, u32[]{:S(2)}) %all-to-all-start) | async-done | bytes 4194336 | tf_op jit(solution)/shard_map/all_to_all | solution.py:30
  115.5 3.1 gather_fusion
  118.6 6.6 %fusion.10 = f32[32,128,256]{2,1,0:T(8,128)} fusion(bf16[1,1,32,256,256]{4,3,2,1,0:T(8,128)(2,1)} %param.8, bf16[32,256,128]{2,1,0:T(8,128)(2,1)S(1)} %gather_fusion, pred[32]{0:T(512)(128)(4,1)S(1)} %compare_and_fusion), kind=kOutput, calls=%fused_computation.13 | convolution fusion | flops 537919488 | bytes 10485792 | tf_op jit(solution)/shard_map/sij,sjk->sik/dot_general | solution.py:35
  125.2 5.5 %copy.9 = f32[32,128,256]{1,0,2:T(8,128)} copy(f32[32,128,256]{2,1,0:T(8,128)} %fusion.10) | data formatting | bytes 8388608 | tf_op jit(solution)/shard_map/sij,sjk->sik/dot_general | solution.py:35
  130.7 4.3 fusion.18
  135.0 1.2 copy.6
  136.3 45.0 %reduce-scatter.4.cloned.1.call-done = bf16[512,128]{1,0:T(8,128)(2,1)} async-done(((bf16[4096,128]{1,0:T(8,128)(2,1)}), bf16[512,128]{1,0:T(8,128)(2,1)}) %reduce-scatter.4.cloned.1.call-update) | async-done | bytes 131088 | tf_op jit(solution)/shard_map/reduce_scatter | solution.py:40
  183.2 101.7 %all_to_all.15 = bf16[32,512,128]{2,1,0:T(8,128)(2,1)} all-to-all(bf16[32,512,128]{2,1,0:T(8,128)(2,1)S(1)} %stack.7), channel_id=1, replica_groups=mesh['row'=32,'col'=8,'vec'=2] {'row'}, dimensions={0} | all-to-all | bytes 8388608 | tf_op jit(solution)/shard_map/all_to_all | solution.py:30
  284.9 3.1 gather_fusion.1
  288.1 6.6 %fusion.8 = f32[32,128,256]{2,1,0:T(8,128)} fusion(bf16[1,1,32,256,256]{4,3,2,1,0:T(8,128)(2,1)} %param.8, bf16[32,256,128]{2,1,0:T(8,128)(2,1)S(1)} %gather_fusion.1, pred[32]{0:T(512)(128)(4,1)S(1)} %compare_and_fusion), kind=kOutput, calls=%fused_computation.11 | convolution fusion | flops 537919488 | bytes 10485792 | tf_op jit(solution)/shard_map/sij,sjk->sik/dot_general | solution.py:35
  294.6 5.5 %copy.10 = f32[32,128,256]{1,0,2:T(8,128)} copy(f32[32,128,256]{2,1,0:T(8,128)} %fusion.8) | data formatting | bytes 8388608 | tf_op jit(solution)/shard_map/sij,sjk->sik/dot_general | solution.py:35
  300.1 4.3 fusion.21
  304.4 1.2 copy.7
  305.9 39.3 %reduce-scatter.6.cloned.1.call-done = bf16[512,128]{1,0:T(8,128)(2,1)} async-done(((bf16[4096,128]{1,0:T(8,128)(2,1)}), bf16[512,128]{1,0:T(8,128)(2,1)}) %reduce-scatter.6.cloned.1.call-update) | async-done | bytes 131088 | tf_op jit(solution)/shard_map/reduce_scatter | solution.py:40
  347.1 101.8 %all_to_all.16 = bf16[32,512,128]{2,1,0:T(8,128)(2,1)} all-to-all(bf16[32,512,128]{2,1,0:T(8,128)(2,1)S(1)} %stack.8), channel_id=1, replica_groups=mesh['row'=32,'col'=8,'vec'=2] {'row'}, dimensions={0} | all-to-all | bytes 8388608 | tf_op jit(solution)/shard_map/all_to_all | solution.py:30
  448.9 3.1 gather_fusion.2
  452.0 6.6 %fusion.6 = f32[32,128,256]{2,1,0:T(8,128)} fusion(bf16[1,1,32,256,256]{4,3,2,1,0:T(8,128)(2,1)} %param.8, bf16[32,256,128]{2,1,0:T(8,128)(2,1)S(1)} %gather_fusion.2, pred[32]{0:T(512)(128)(4,1)S(1)} %compare_and_fusion), kind=kOutput, calls=%fused_computation.9 | convolution fusion | flops 537919488 | bytes 10485792 | tf_op jit(solution)/shard_map/sij,sjk->sik/dot_general | solution.py:35
  458.6 5.5 %copy.11 = f32[32,128,256]{1,0,2:T(8,128)} copy(f32[32,128,256]{2,1,0:T(8,128)} %fusion.6) | data formatting | bytes 8388608 | tf_op jit(solution)/shard_map/sij,sjk->sik/dot_general | solution.py:35
  464.1 4.3 fusion.24
  468.4 1.2 copy.8
  469.6 39.7 %reduce-scatter.8.cloned.1.call-done = bf16[512,128]{1,0:T(8,128)(2,1)} async-done(((bf16[4096,128]{1,0:T(8,128)(2,1)}), bf16[512,128]{1,0:T(8,128)(2,1)}) %reduce-scatter.8.cloned.1.call-update) | async-done | bytes 131088 | tf_op jit(solution)/shard_map/reduce_scatter | solution.py:40
  509.3 1.6 fusion.35
  (20 shorter events, 4.2 us)
Async XLA Ops:
  10.4 11.2 %copy-start.2 = (s32[1,1,32]{2,1,0:T(1,128)S(1)}, s32[1,1,32]{2,1,0:T(1,128)}, u32[]{:S(2)}) copy-start(s32[1,1,32]{2,1,0:T(1,128)} %param.10) | copy-start | bytes 388
  10.4 105.1 %all-to-all-start = ((bf16[32,512,128]{2,1,0:T(8,128)(2,1)}), bf16[32,512,128]{2,1,0:T(8,128)(2,1)}, u32[]{:S(2)}, u32[]{:S(2)}) async-start(bf16[32,512,128]{2,1,0:T(8,128)(2,1)} %stack.6), calls=%async_computation | async-start | bytes 8388608 | tf_op jit(solution)/shard_map/all_to_all | solution.py:30
  20.9 160.4 %reduce-scatter.4.cloned.1.call-start = ((), (), s32[]{:S(2)}) async-start(), calls=%async_computation.6 | async-start | bytes 1179648 | tf_op jit(solution)/shard_map/reduce_scatter | solution.py:40
  125.2 5.5 %copy-start.1 = (s32[1,1,32]{2,1,0:T(1,128)S(1)}, s32[1,1,32]{2,1,0:T(1,128)}, u32[]{:S(2)}) copy-start(s32[1,1,32]{2,1,0:T(1,128)} %param.9) | copy-start | bytes 388
  130.7 50.6 %copy-start = (bf16[512,128]{1,0:T(8,128)(2,1)S(1)}, bf16[512,128]{1,0:T(8,128)(2,1)}, u32[]{:S(2)}) copy-start(bf16[512,128]{1,0:T(8,128)(2,1)} %param.7) | copy-start | bytes 393220
  136.3 208.9 %reduce-scatter.6.cloned.1.call-start = ((), (), s32[]{:S(2)}) async-start(), calls=%async_computation.7 | async-start | bytes 1179648 | tf_op jit(solution)/shard_map/reduce_scatter | solution.py:40
  305.7 203.7 %reduce-scatter.8.cloned.1.call-start = ((), (), s32[]{:S(2)}) async-start(), calls=%async_computation.8 | async-start | bytes 1179648 | tf_op jit(solution)/shard_map/reduce_scatter | solution.py:40
Sparse Core Ops, SparseCore 0:
  136.4 44.8 reduce-scatter.3
  305.8 39.3 reduce-scatter.5
  469.8 39.4 reduce-scatter.7
